TPU v7x, 512 devices: a whole 4x8x8 slice. The times are simulated.
512 devices in a mesh: inner: 32 (over z_lo, y, core), outer: 16 (over x, z_hi).
Axes of the slice: x: 4, y: 8, z: 8 (z_hi: 4, z_lo: 2; z = z_hi * 2 + z_lo), core: 2. Of those that a mesh axis runs over, the one named last changes fastest.
Arguments:
- gradients: bfloat16 [32, 16, 256, 8192], P('inner', 'outer'), may hold values from -6 to 6
- master_shard: float32 [256, 8192], P('outer', 'inner'), may hold values from -6 to 6
- first_moment: float32 [256, 8192], P('outer', 'inner'), may hold values from -48 to 48
- second_moment: float32 [256, 8192], P('outer', 'inner'), may hold values from 100 to 1000
Outputs:
- new_master: float32 [256, 8192], P('outer', 'inner')
- new_first: float32 [256, 8192], P('outer', 'inner')
- new_second: float32 [256, 8192], P('outer', 'inner')
- group_weights: bfloat16 [256, 8192], P(None, 'inner')
All inputs are finite; a program needn't handle non-finite values.
Results may differ from a plain program's by a relative error of at most 0.0025.
Values may be sent and summed in bfloat16 or wider, within the bound.
A program may use at most 64 MiB of HBM per device.

v0:
```python
import jax
import jax.numpy as jnp
from jax import lax
from jax.sharding import PartitionSpec as P

beta_first = 0.9
beta_second = 0.95
learn_rate = 0.05
decay_rate = 0.1
adam_eps = 1e-05
bias_first = 1.0 - 0.9**10
bias_second = 1.0 - 0.95**10


def sum_sources(pieces):
    return jnp.sum(pieces.astype(jnp.float32), axis=0)


def body(gradients, master_shard, first_moment, second_moment):
    local = gradients.reshape(1, gradients.shape[2], gradients.shape[3])
    partial_value = sum_sources(
        lax.all_to_all(local, "inner", split_axis=2, concat_axis=0, tiled=True)
    )
    reduced = sum_sources(
        lax.all_to_all(
            partial_value[None].astype(jnp.bfloat16),
            "outer",
            split_axis=1,
            concat_axis=0,
            tiled=True,
        ).astype(jnp.float32)
    )
    new_first = beta_first * first_moment + (1.0 - beta_first) * reduced
    new_second = beta_second * second_moment + (1.0 - beta_second) * reduced * reduced
    update = (
        new_first / bias_first / (jnp.sqrt(new_second / bias_second) + adam_eps)
        + decay_rate * master_shard
    )
    new_master = master_shard - learn_rate * update
    copy_weights = lax.all_gather(new_master.astype(jnp.bfloat16), "outer", axis=0, tiled=True)
    return (new_master, new_first, new_second, copy_weights)


def solution(mesh):
    return jax.shard_map(
        body,
        mesh=mesh,
        in_specs=(
            P("inner", "outer", None, None),
            P("outer", "inner"),
            P("outer", "inner"),
            P("outer", "inner"),
        ),
        out_specs=(P("outer", "inner"), P("outer", "inner"), P("outer", "inner"), P(None, "inner")),
        check_vma=False,
    )
```

profile of v0, /device:TPU:8, one launch (start us, length us, event | category | flops | bytes accessed | tf_op | source)
XLA Modules:
  0.0 269.7 jit_solution(8920335155351503580)
XLA Ops:
  0.6 17.9 %copy.11 = bf16[1,256,8192]{1,0,2:T(2,128)(2,1)} copy(bf16[1,256,8192]{2,1,0:T(8,128)(2,1)} %bitcast.11) | data formatting | bytes 8388608 | tf_op jit(solution)/shard_map/reshape | solution.py:20
  18.5 0.5 broadcast.18
  19.0 43.5 %reduce.4 = bf16[8192,256]{1,0:T(8,128)(2,1)} reduce(bf16[8192,1,256]{2,1,0:T(2,128)(2,1)} %bitcast.8, bf16[]{:T(256)} %broadcast.18), dimensions={1}, to_apply=%bitcast.4.reduce_sub_computation | reduce | bytes 8388610
  62.5 6.9 %reshape.29 = bf16[32,2,32768]{2,1,0:T(2,128)(2,1)} reshape(bf16[8192,256]{1,0:T(8,128)(2,1)} %reduce.4) | data formatting | bytes 8388608
  69.4 106.8 %all_to_all.21 = bf16[32,2,32768]{2,1,0:T(2,128)(2,1)} all-to-all(bf16[32,2,32768]{2,1,0:T(2,128)(2,1)} %reshape.29), channel_id=1, replica_groups=mesh['inner'=32,'outer'=16] {'inner'}, dimensions={0} | all-to-all | bytes 8388608 | tf_op jit(solution)/shard_map/all_to_all | solution.py:22
  176.2 19.8 %reshape.30 = bf16[8192,1,256]{2,1,0:T(2,128)(2,1)} reshape(bf16[32,2,32768]{2,1,0:T(2,128)(2,1)} %all_to_all.21) | data formatting | bytes 8388608
  196.0 6.1 %copy.16 = bf16[1,256,8192]{1,2,0:T(8,128)(2,1)} copy(bf16[1,256,8192]{1,0,2:T(2,128)(2,1)} %bitcast.9) | data formatting | bytes 8388608
  202.1 0.0 copy-start
  202.1 0.0 copy-start.1
  202.1 0.0 copy-start.2
  202.1 2.8 %reduce_sum.21 = bf16[256,256]{0,1:T(8,128)(2,1)S(1)} reduce(bf16[256,32,256]{0,2,1:T(8,128)(2,1)} %bitcast.10, bf16[]{:T(256)} %constant.4.clone.1), dimensions={1}, to_apply=%region_0.0 | reduce | flops 2031616 | bytes 4325378 | tf_op jit(solution)/shard_map/reduce_sum | solution.py:16
  204.9 0.2 copy.13
  205.1 1.4 reduce.5
  206.6 21.7 %all_to_all.22 = bf16[16,2,2048]{2,1,0:T(2,128)(2,1)S(1)} all-to-all(bf16[16,2,2048]{2,1,0:T(2,128)(2,1)S(1)} %reshape.31), channel_id=1, replica_groups=mesh['inner'=32,'outer'=16] {'outer'}, dimensions={0} | all-to-all | bytes 262144 | tf_op jit(solution)/shard_map/all_to_all | solution.py:25
  228.3 0.1 reshape.32
  228.5 0.0 copy-done
  228.5 0.0 copy-done.1
  228.5 0.0 copy-done.2
  228.5 0.6 fusion.1
  229.1 39.9 %all_gather.3 = bf16[256,256]{1,0:T(8,128)(2,1)S(1)} all-gather(bf16[16,256]{1,0:T(8,128)(2,1)S(1)} %get-tuple-element.4), channel_id=1, replica_groups=mesh['inner'=32,'outer'=16] {'outer'}, dimensions={0}, use_global_device_ids=true | all-gather | bytes 139264 | tf_op jit(solution)/shard_map/all_gather | solution.py:40
  269.0 0.7 copy.19
  (3 shorter events, 0.1 us)
Async XLA Ops:
  202.1 26.4 %copy-start = (f32[16,256]{1,0:T(8,128)S(1)}, f32[16,256]{1,0:T(8,128)}, u32[]{:S(2)}) copy-start(f32[16,256]{1,0:T(8,128)} %param.5) | copy-start | bytes 49156
  202.1 26.4 %copy-start.1 = (f32[16,256]{1,0:T(8,128)S(1)}, f32[16,256]{1,0:T(8,128)}, u32[]{:S(2)}) copy-start(f32[16,256]{1,0:T(8,128)} %param.6) | copy-start | bytes 49156
  202.1 26.4 %copy-start.2 = (f32[16,256]{1,0:T(8,128)S(1)}, f32[16,256]{1,0:T(8,128)}, u32[]{:S(2)}) copy-start(f32[16,256]{1,0:T(8,128)} %param.7) | copy-start | bytes 49156
where the time goes:
time: 271 us; the launch traced here: 270 us
  blocking collectives  168 us (62%)
  local copies, waits for them, and re-layouts  52.1 us (19%)
  other arithmetic  48.4 us (18%)
    all_to_all x1, blocking collectives, body(): lax.all_to_all(local, 'inner', split_axis=2, concat_axis=0, tiled=True)  107 us
    unnamed x2, other arithmetic  44.9 us
    all_gather x1, blocking collectives, body(): lax.all_gather(new_master.astype(jnp.bfloat16), 'outer', axis=0, tiled=True)  39.9 us
    unnamed x14, local copies, waits for them, and re-layouts  34.1 us
    all_to_all x1, blocking collectives, body(): lax.all_to_all(partial_value[None].astype(jnp.bfloat16), 'outer', split_a...  21.7 us
    reshape x1, local copies, waits for them, and re-layouts, body(): local = gradients.reshape(1, gradients.shape[2], gradients.shape[3])  17.9 us

commit v1 on v0

--- a/solution.py
+++ b/solution.py
@@ -19,7 +19,12 @@
 def body(gradients, master_shard, first_moment, second_moment):
     local = gradients.reshape(1, gradients.shape[2], gradients.shape[3])
     partial_value = sum_sources(
-        lax.all_to_all(local, "inner", split_axis=2, concat_axis=0, tiled=True)
+        jnp.concatenate(
+            lax.all_to_all(
+                jnp.stack(jnp.split(local, lax.axis_size("inner"), axis=2)), "inner", 0, 0
+            ),
+            axis=0,
+        )
     )
     reduced = sum_sources(
         lax.all_to_all(

time: 271 us -> 191 us (0.70)
  other arithmetic: 48.4 us -> 4.88 us
  local copies, waits for them, and re-layouts: 52.1 us -> 16.9 us
    unnamed x2 -> x1, other arithmetic: 44.9 us -> 1.41 us
    reshape x1 -> x0, local copies, waits for them, and re-layouts: 17.9 us -> none  [body(): local = gradients.reshape(1, gradients.shape[2], gradients.shape[3])]
    unnamed x14 -> x44, local copies, waits for them, and re-layouts: 34.1 us -> 16.7 us
where the time goes in v1:
time: 191 us
  blocking collectives  168 us (88%)
  local copies, waits for them, and re-layouts  16.9 us (9%)
  other arithmetic  4.88 us (3%)
    all_to_all x1, blocking collectives, body(): lax.all_to_all(jnp.stack(jnp.split(local, lax.axis_size('inner'), axis=2)...  106 us
    all_gather x1, blocking collectives, body(): lax.all_gather(new_master.astype(jnp.bfloat16), 'outer', axis=0, tiled=True)  39.9 us
    all_to_all x1, blocking collectives, body(): lax.all_to_all(partial_value[None].astype(jnp.bfloat16), 'outer', split_a...  22.5 us
    unnamed x44, local copies, waits for them, and re-layouts  16.7 us

profile of v1, /device:TPU:8, one launch (start us, length us, event | category | flops | bytes accessed | tf_op | source)
XLA Modules:
  0.0 190.9 jit_solution(15432516116507488973)
XLA Ops:
  0.6 0.0 copy-start
  0.6 1.1 fusion.31
  1.7 1.2 fusion.30
  2.9 0.9 fusion.29
  3.8 0.9 fusion.28
  4.7 0.9 fusion.27
  5.6 0.9 fusion.26
  6.6 0.9 fusion.25
  7.5 0.9 fusion.24
  8.4 0.9 fusion.23
  9.3 0.9 fusion.22
  10.2 0.9 fusion.21
  11.2 0.9 fusion.20
  12.1 0.9 fusion.19
  13.0 0.9 fusion.18
  13.9 0.9 fusion.17
  14.8 0.9 fusion.16
  15.8 0.0 copy-done
  16.2 105.8 %all_to_all.14 = bf16[32,1,256,256]{3,2,1,0:T(8,128)(2,1)} all-to-all(bf16[32,1,256,256]{3,2,1,0:T(8,128)(2,1)S(1)} %fusion), channel_id=1, replica_groups=mesh['inner'=32,'outer'=16] {'inner'}, dimensions={0} | all-to-all | bytes 8388608 | tf_op jit(solution)/shard_map/all_to_all | solution.py:23
  122.0 0.0 copy-start.1
  122.0 0.0 copy-start.2
  122.0 0.0 copy-start.3
  122.0 2.8 %reduce_sum.21 = bf16[256,256]{1,0:T(8,128)(2,1)S(1)} reduce(bf16[32,1,256,256]{3,2,1,0:T(8,128)(2,1)} %all_to_all.14, bf16[]{:T(256)} %constant.4.clone.1), dimensions={0,1}, to_apply=%region_0.0 | reduce | flops 2031616 | bytes 4325378 | tf_op jit(solution)/shard_map/reduce_sum | solution.py:16
  124.9 0.2 copy.11
  125.1 0.5 broadcast.18
  125.6 1.4 reduce.2
  127.0 22.5 %all_to_all.15 = bf16[16,2,2048]{2,1,0:T(2,128)(2,1)S(1)} all-to-all(bf16[16,2,2048]{2,1,0:T(2,128)(2,1)S(1)} %reshape.29), channel_id=1, replica_groups=mesh['inner'=32,'outer'=16] {'outer'}, dimensions={0} | all-to-all | bytes 262144 | tf_op jit(solution)/shard_map/all_to_all | solution.py:30
  149.5 0.1 reshape.30
  149.7 0.0 copy-done.1
  149.7 0.0 copy-done.2
  149.8 0.0 copy-done.3
  149.8 0.6 fusion.33
  150.4 39.9 %all_gather.3 = bf16[256,256]{1,0:T(8,128)(2,1)S(1)} all-gather(bf16[16,256]{1,0:T(8,128)(2,1)S(1)} %get-tuple-element.4), channel_id=1, replica_groups=mesh['inner'=32,'outer'=16] {'outer'}, dimensions={0}, use_global_device_ids=true | all-gather | bytes 139264 | tf_op jit(solution)/shard_map/all_gather | solution.py:45
  190.3 0.7 copy.44
  (19 shorter events, 0.4 us)
Async XLA Ops:
  0.6 15.1 %copy-start = (bf16[1,1,256,8192]{3,2,1,0:T(8,128)(2,1)S(1)}, bf16[1,1,256,8192]{3,2,1,0:T(8,128)(2,1)}, u32[]{:S(2)}) copy-start(bf16[1,1,256,8192]{3,2,1,0:T(8,128)(2,1)} %param.4) | copy-start | bytes 12582916
  122.0 27.7 %copy-start.1 = (f32[16,256]{1,0:T(8,128)S(1)}, f32[16,256]{1,0:T(8,128)}, u32[]{:S(2)}) copy-start(f32[16,256]{1,0:T(8,128)} %param.5) | copy-start | bytes 49156
  122.0 27.7 %copy-start.2 = (f32[16,256]{1,0:T(8,128)S(1)}, f32[16,256]{1,0:T(8,128)}, u32[]{:S(2)}) copy-start(f32[16,256]{1,0:T(8,128)} %param.6) | copy-start | bytes 49156
  122.0 27.7 %copy-start.3 = (f32[16,256]{1,0:T(8,128)S(1)}, f32[16,256]{1,0:T(8,128)}, u32[]{:S(2)}) copy-start(f32[16,256]{1,0:T(8,128)} %param.7) | copy-start | bytes 49156
